TPU v7x, 32 devices: a whole 2x2x4 slice. The times are simulated.
32 devices in a mesh: region: 2 (over x), rows: 8 (over z, y), section: 2 (over core).
Axes of the slice: x: 2, y: 2, z: 4, core: 2. Of those that a mesh axis runs over, the one named last changes fastest.
Arguments:
- transitions: float32 [4, 4, 4096, 4096], P(('region', 'section'), None, 'rows'), parts along dimension 0, may hold values from 0 to 1, as said below
- gain: float32 [4, 4, 4096], P(('region', 'section'), None, 'rows'), parts along dimension 0, may hold values from 0 to 1
- cost: float32 [4, 4, 8], P(('region', 'section')), parts along dimension 0, may hold values from 0 to 1
- price_class: int32 [2048], P('region'), parts along dimension 0, may hold values from 0 to 7
- terminal: float32 [8192, 1024], P(('region', 'rows')), parts along dimension 0, may hold values from 0.5 to 3.5
Outputs:
- values: float32 [4, 4096, 1024], P(('region', 'section'), 'rows'), parts along dimension 0
There are 2 independent parts, one for each index of `region`. A program takes and returns all parts, laid end to end along the dimension named above; each array names one. Nothing has to cross between parts.
Inputs may be any that keep to these rules, and one draw needn't show every extreme that they name: `transitions`: entries are nonnegative.
All inputs are finite; a program needn't handle non-finite values.
Results may differ from a plain program's by a relative error of at most 0.0001.
Values sent between devices are 32-bit elements; how exact they have to be, the bound alone decides.
No kernel may reach another device: no remote copies, remote signals or barrier semaphores. Data moves between devices by JAX's collectives and lax.ppermute only.
A program may use at most 128 MiB of HBM per device.

v0:
```python
import jax
import jax.numpy as jnp
from jax import lax
from jax.sharding import PartitionSpec as P


def from_behind(value, axis, by):
    size = lax.axis_size(axis)
    pairs = [(i, i + by) for i in range(size) if 0 <= i + by < size]
    return lax.ppermute(value, axis, pairs)


def shards(transitions, gain, cost, price_class, terminal):
    num_groups = lax.axis_size("section")
    my_group = lax.axis_index("section")
    kernel = transitions[0]
    action_count, rows_here, state_count = kernel.shape
    scenarios = terminal.shape[1]
    price_levels = cost.shape[2]
    batch_count = 4
    batch_width = scenarios // batch_count
    levels = jnp.arange(price_levels, dtype=jnp.int32)
    onehot = (price_class[None, :] == levels[:, None]).astype(jnp.float32)
    charge = jnp.dot(cost[0], onehot, precision=lax.Precision.HIGHEST)
    gains = gain[0]
    is_last = my_group == num_groups - 1

    def accumulate(panel):
        return jnp.einsum(
            "arn,nc->arc",
            kernel,
            panel,
            precision=lax.Precision.HIGHEST,
            preferred_element_type=jnp.float32,
        )

    def advance(step_index, carry):
        incoming, results = carry
        batch_index = step_index - (num_groups - 1 - my_group)
        is_live = (batch_index >= 0) & (batch_index < batch_count)
        clamped = jnp.clip(batch_index, 0, batch_count - 1)
        first_col = clamped * batch_width
        from_end = lax.dynamic_slice_in_dim(terminal, first_col, batch_width, 1)
        current = jnp.where(is_last, from_end, incoming)
        summed = accumulate(lax.all_gather(current, "rows", axis=0, tiled=True))
        batch_charge = lax.dynamic_slice_in_dim(charge, first_col, batch_width, 1)
        action_value = summed + gains[:, :, None] - batch_charge[:, None, :]
        values_now = jnp.max(action_value, axis=0)
        previous = lax.dynamic_slice_in_dim(results, first_col, batch_width, 1)
        results = lax.dynamic_update_slice_in_dim(
            results, jnp.where(is_live, values_now, previous), first_col, 1
        )
        handed = from_behind(values_now, "section", -1)
        return (handed, results)

    step_total = batch_count + num_groups - 1
    start_carry = (
        jnp.zeros((rows_here, batch_width), jnp.float32),
        jnp.zeros((rows_here, scenarios), jnp.float32),
    )
    final_carry = lax.fori_loop(0, step_total, advance, start_carry)
    return final_carry[1][None]


def solution(mesh):
    return jax.shard_map(
        shards,
        mesh=mesh,
        in_specs=(
            P(("region", "section"), None, "rows", None),
            P(("region", "section"), None, "rows"),
            P(("region", "section"), None, None),
            P("region"),
            P(("region", "rows"), None),
        ),
        out_specs=P(("region", "section"), "rows", None),
        check_vma=False,
    )
```

profile of v0, /device:TPU:1, one launch (start us, length us, event | category | flops | bytes accessed | tf_op | source)
XLA Modules:
  0.0 578.3 jit_solution(10681932668837966376)
XLA Ops:
  6.5 0.7 copy-done
  7.2 0.8 convolution_bitcast_fusion
  8.1 1.6 broadcast_in_dim.15.clone
  9.7 562.0 %while.17 = (s32[]{:T(128)}, f32[512,256]{0,1:T(8,128)S(1)}, f32[512,1024]{1,0:T(8,128)}, pred[]{:T(512)}, s32[]{:T(128)}, /*index=5*/f32[512,1024]{1,0:T(8,128)...) while((s32[]{:T(128)}, f32[512,256]{0,1:T(8,128)S(1)}, ...), condition=%wide.region_2.3_spmd, body=%wide.region_0.2_spmd.sunk | while | flops 25771507712 | bytes 63983956 | solution.py:61
  9.7 1.1 constant_dynamic-slice_fusion.6
  11.0 0.9 broadcast_select_fusion.4
  11.9 75.1 %all-gather.2.cloned.1.call-done = f32[4096,256]{0,1:T(8,128)} async-done(((f32[512,256]{0,1:T(8,128)}), f32[4096,256]{0,1:T(8,128)}) %all-gather.2.cloned.1.call-update) | async-done | bytes 4194320 | tf_op jit(solution)/shard_map/while/body/eval_jaxpr/all_gather | solution.py:45
  87.0 32.4 %fusion.13 = f32[512,256]{0,1:T(8,128)S(1)} fusion(f32[4,512,4096]{2,1,0:T(8,128)} %get-tuple-element.345, f32[4096,256]{0,1:T(8,128)} %all-gather.2.cloned.1.call-done, f32[4,256]{1,0:T(4,128)S(1)} %constant_dynamic-slice_fusion.7, f32[4,512]{1,0:T(4,128)S(1)} %bitcast.27), kind=kOutput, calls=%fused_computation.3.clone.1 | convolution fusion | flops 25771245568 | bytes 38285312 | tf_op jit(solution)/shard_map/while/body/eval_jaxpr/arn,nc->arc/dot_general | solution.py:29
  119.4 3.8 collective-permute-start
  123.3 1.1 constant_dynamic-slice_fusion.8
  124.6 0.2 copy.19
  124.8 0.8 constant_dynamic-update-slice_fusion.2
  125.7 1.1 constant_dynamic-slice_fusion.6
  126.8 0.2 copy.17
  127.0 0.9 broadcast_select_fusion.4
  127.9 70.8 %all-gather.2.cloned.1.call-done = f32[4096,256]{0,1:T(8,128)} async-done(((f32[512,256]{0,1:T(8,128)}), f32[4096,256]{0,1:T(8,128)}) %all-gather.2.cloned.1.call-update) | async-done | bytes 4194320 | tf_op jit(solution)/shard_map/while/body/eval_jaxpr/all_gather | solution.py:45
  198.7 32.4 %fusion.13 = f32[512,256]{0,1:T(8,128)S(1)} fusion(f32[4,512,4096]{2,1,0:T(8,128)} %get-tuple-element.345, f32[4096,256]{0,1:T(8,128)} %all-gather.2.cloned.1.call-done, f32[4,256]{1,0:T(4,128)S(1)} %constant_dynamic-slice_fusion.7, f32[4,512]{1,0:T(4,128)S(1)} %bitcast.27), kind=kOutput, calls=%fused_computation.3.clone.1 | convolution fusion | flops 25771245568 | bytes 38285312 | tf_op jit(solution)/shard_map/while/body/eval_jaxpr/arn,nc->arc/dot_general | solution.py:29
  231.1 3.8 collective-permute-start
  234.9 1.1 constant_dynamic-slice_fusion.8
  236.0 0.2 copy.18
  236.3 0.2 copy.19
  236.5 0.8 constant_dynamic-update-slice_fusion.2
  237.4 1.1 constant_dynamic-slice_fusion.6
  238.4 0.2 copy.17
  238.6 0.9 broadcast_select_fusion.4
  239.6 70.8 %all-gather.2.cloned.1.call-done = f32[4096,256]{0,1:T(8,128)} async-done(((f32[512,256]{0,1:T(8,128)}), f32[4096,256]{0,1:T(8,128)}) %all-gather.2.cloned.1.call-update) | async-done | bytes 4194320 | tf_op jit(solution)/shard_map/while/body/eval_jaxpr/all_gather | solution.py:45
  310.3 32.4 %fusion.13 = f32[512,256]{0,1:T(8,128)S(1)} fusion(f32[4,512,4096]{2,1,0:T(8,128)} %get-tuple-element.345, f32[4096,256]{0,1:T(8,128)} %all-gather.2.cloned.1.call-done, f32[4,256]{1,0:T(4,128)S(1)} %constant_dynamic-slice_fusion.7, f32[4,512]{1,0:T(4,128)S(1)} %bitcast.27), kind=kOutput, calls=%fused_computation.3.clone.1 | convolution fusion | flops 25771245568 | bytes 38285312 | tf_op jit(solution)/shard_map/while/body/eval_jaxpr/arn,nc->arc/dot_general | solution.py:29
  342.8 3.8 collective-permute-start
  346.6 1.1 constant_dynamic-slice_fusion.8
  347.7 0.2 copy.18
  348.0 0.2 copy.19
  348.2 0.8 constant_dynamic-update-slice_fusion.2
  349.0 1.1 constant_dynamic-slice_fusion.6
  350.1 0.2 copy.17
  350.3 0.9 broadcast_select_fusion.4
  351.2 70.4 %all-gather.2.cloned.1.call-done = f32[4096,256]{0,1:T(8,128)} async-done(((f32[512,256]{0,1:T(8,128)}), f32[4096,256]{0,1:T(8,128)}) %all-gather.2.cloned.1.call-update) | async-done | bytes 4194320 | tf_op jit(solution)/shard_map/while/body/eval_jaxpr/all_gather | solution.py:45
  421.7 32.4 %fusion.13 = f32[512,256]{0,1:T(8,128)S(1)} fusion(f32[4,512,4096]{2,1,0:T(8,128)} %get-tuple-element.345, f32[4096,256]{0,1:T(8,128)} %all-gather.2.cloned.1.call-done, f32[4,256]{1,0:T(4,128)S(1)} %constant_dynamic-slice_fusion.7, f32[4,512]{1,0:T(4,128)S(1)} %bitcast.27), kind=kOutput, calls=%fused_computation.3.clone.1 | convolution fusion | flops 25771245568 | bytes 38285312 | tf_op jit(solution)/shard_map/while/body/eval_jaxpr/arn,nc->arc/dot_general | solution.py:29
  454.1 3.8 collective-permute-start
  457.9 1.1 constant_dynamic-slice_fusion.8
  459.3 0.2 copy.19
  459.5 0.8 constant_dynamic-update-slice_fusion.2
  460.4 1.1 constant_dynamic-slice_fusion.6
  461.7 0.9 broadcast_select_fusion.4
  462.6 70.4 %all-gather.2.cloned.1.call-done = f32[4096,256]{0,1:T(8,128)} async-done(((f32[512,256]{0,1:T(8,128)}), f32[4096,256]{0,1:T(8,128)}) %all-gather.2.cloned.1.call-update) | async-done | bytes 4194320 | tf_op jit(solution)/shard_map/while/body/eval_jaxpr/all_gather | solution.py:45
  533.0 32.4 %fusion.13 = f32[512,256]{0,1:T(8,128)S(1)} fusion(f32[4,512,4096]{2,1,0:T(8,128)} %get-tuple-element.345, f32[4096,256]{0,1:T(8,128)} %all-gather.2.cloned.1.call-done, f32[4,256]{1,0:T(4,128)S(1)} %constant_dynamic-slice_fusion.7, f32[4,512]{1,0:T(4,128)S(1)} %bitcast.27), kind=kOutput, calls=%fused_computation.3.clone.1 | convolution fusion | flops 25771245568 | bytes 38285312 | tf_op jit(solution)/shard_map/while/body/eval_jaxpr/arn,nc->arc/dot_general | solution.py:29
  565.5 3.8 collective-permute-start
  569.3 1.1 constant_dynamic-slice_fusion.8
  570.9 0.8 constant_dynamic-update-slice_fusion.2
  (35 shorter events, 1.8 us)
Async XLA Ops:
  6.5 0.7 copy-start
  6.5 3.1 copy-start.1
  9.7 77.3 %all-gather.2.cloned.1.call-start = ((), (), s32[]{:S(2)}) async-start(), calls=%async_computation | async-start | bytes 4718592 | tf_op jit(solution)/shard_map/while/body/eval_jaxpr/all_gather | solution.py:45
  119.4 6.2 %collective-permute-start = (f32[512,256]{0,1:T(8,128)S(1)}, f32[512,256]{0,1:T(8,128)S(1)}, u32[]{:S(2)}, u32[]{:S(2)}) collective-permute-start(f32[512,256]{0,1:T(8,128)S(1)} %fusion.13), channel_id=1, source_target_pairs={{1,0},{3,2},{5,4},{7,6},{9,8},{11,10},{13,12},{15,14},{17,16},{19,... | collective-permute-start | bytes 1572872 | tf_op jit(solution)/shard_map/while/body/eval_jaxpr/ppermute | solution.py:10
  125.7 73.0 %all-gather.2.cloned.1.call-start = ((), (), s32[]{:S(2)}) async-start(), calls=%async_computation | async-start | bytes 4718592 | tf_op jit(solution)/shard_map/while/body/eval_jaxpr/all_gather | solution.py:45
  231.1 6.2 %collective-permute-start = (f32[512,256]{0,1:T(8,128)S(1)}, f32[512,256]{0,1:T(8,128)S(1)}, u32[]{:S(2)}, u32[]{:S(2)}) collective-permute-start(f32[512,256]{0,1:T(8,128)S(1)} %fusion.13), channel_id=1, source_target_pairs={{1,0},{3,2},{5,4},{7,6},{9,8},{11,10},{13,12},{15,14},{17,16},{19,... | collective-permute-start | bytes 1572872 | tf_op jit(solution)/shard_map/while/body/eval_jaxpr/ppermute | solution.py:10
  237.4 73.0 %all-gather.2.cloned.1.call-start = ((), (), s32[]{:S(2)}) async-start(), calls=%async_computation | async-start | bytes 4718592 | tf_op jit(solution)/shard_map/while/body/eval_jaxpr/all_gather | solution.py:45
  342.8 6.2 %collective-permute-start = (f32[512,256]{0,1:T(8,128)S(1)}, f32[512,256]{0,1:T(8,128)S(1)}, u32[]{:S(2)}, u32[]{:S(2)}) collective-permute-start(f32[512,256]{0,1:T(8,128)S(1)} %fusion.13), channel_id=1, source_target_pairs={{1,0},{3,2},{5,4},{7,6},{9,8},{11,10},{13,12},{15,14},{17,16},{19,... | collective-permute-start | bytes 1572872 | tf_op jit(solution)/shard_map/while/body/eval_jaxpr/ppermute | solution.py:10
  349.0 72.7 %all-gather.2.cloned.1.call-start = ((), (), s32[]{:S(2)}) async-start(), calls=%async_computation | async-start | bytes 4718592 | tf_op jit(solution)/shard_map/while/body/eval_jaxpr/all_gather | solution.py:45
  454.1 6.2 %collective-permute-start = (f32[512,256]{0,1:T(8,128)S(1)}, f32[512,256]{0,1:T(8,128)S(1)}, u32[]{:S(2)}, u32[]{:S(2)}) collective-permute-start(f32[512,256]{0,1:T(8,128)S(1)} %fusion.13), channel_id=1, source_target_pairs={{1,0},{3,2},{5,4},{7,6},{9,8},{11,10},{13,12},{15,14},{17,16},{19,... | collective-permute-start | bytes 1572872 | tf_op jit(solution)/shard_map/while/body/eval_jaxpr/ppermute | solution.py:10
  460.4 72.7 %all-gather.2.cloned.1.call-start = ((), (), s32[]{:S(2)}) async-start(), calls=%async_computation | async-start | bytes 4718592 | tf_op jit(solution)/shard_map/while/body/eval_jaxpr/all_gather | solution.py:45
  565.5 6.2 %collective-permute-start = (f32[512,256]{0,1:T(8,128)S(1)}, f32[512,256]{0,1:T(8,128)S(1)}, u32[]{:S(2)}, u32[]{:S(2)}) collective-permute-start(f32[512,256]{0,1:T(8,128)S(1)} %fusion.13), channel_id=1, source_target_pairs={{1,0},{3,2},{5,4},{7,6},{9,8},{11,10},{13,12},{15,14},{17,16},{19,... | collective-permute-start | bytes 1572872 | tf_op jit(solution)/shard_map/while/body/eval_jaxpr/ppermute | solution.py:10
Sparse Core Ops, SparseCore 0:
  12.7 74.2 all-gather.1
  128.7 69.9 all-gather.1
  240.4 69.9 all-gather.1
  351.7 69.9 all-gather.1
  463.1 69.9 all-gather.1
where the time goes:
time: 579 us; the launch traced here: 578 us
  waiting for transfers between devices  358 us (62%)
  matrix products  163 us (28%)
  local copies, waits for them, and re-layouts  20.3 us (4%)
  starting transfers between devices  19 us (3%)
  between operations  13.1 us (2%)
    all_gather x5, waiting for transfers between devices, advance(): summed = accumulate(lax.all_gather(current, 'rows', axis=0, tiled=True))  357 us
    dot_general x5, matrix products, accumulate(): jnp.einsum('arn,nc->arc', kernel, panel, precision=lax.Precision.HIGHEST,...  162 us
    ppermute x5, starting transfers between devices, from_behind(): return lax.ppermute(value, axis, pairs)  19 us
  transfers between devices with their start and end apart: 10, of which 5 were waited for; matrix products, arithmetic and copies ran while one was open for 2% of the time, Pallas kernels for 0%

commit v1 on v0

--- a/solution.py
+++ b/solution.py
@@ -2,6 +2,19 @@
 import jax.numpy as jnp
 from jax import lax
 from jax.sharding import PartitionSpec as P
+
+
+def ring_gather(array, axis, dim):
+    ways = lax.axis_size(axis)
+    up = [(d, (d + 1) % ways) for d in range(ways)]
+    down = [(d, (d - 1) % ways) for d in range(ways)]
+    earlier, later = ([array], [array])
+    for _ in range(ways // 2):
+        earlier.append(lax.ppermute(earlier[-1], axis, up))
+    for _ in range((ways - 1) // 2):
+        later.append(lax.ppermute(later[-1], axis, down))
+    line = jnp.concatenate([*earlier[::-1], *later[1:]], axis=dim)
+    return jnp.roll(line, (lax.axis_index(axis) - ways // 2) * array.shape[dim], axis=dim)
 
 
 def from_behind(value, axis, by):
@@ -42,7 +55,7 @@
         first_col = clamped * batch_width
         from_end = lax.dynamic_slice_in_dim(terminal, first_col, batch_width, 1)
         current = jnp.where(is_last, from_end, incoming)
-        summed = accumulate(lax.all_gather(current, "rows", axis=0, tiled=True))
+        summed = accumulate(ring_gather(current, "rows", 0))
         batch_charge = lax.dynamic_slice_in_dim(charge, first_col, batch_width, 1)
         action_value = summed + gains[:, :, None] - batch_charge[:, None, :]
         values_now = jnp.max(action_value, axis=0)

time: 579 us -> 664 us (1.15)
  starting transfers between devices: 19 us -> 107 us
  local copies, waits for them, and re-layouts: 20.3 us -> 34.4 us
  between operations: 13.1 us -> 0.01 us
    all_gather x5 -> x0, waiting for transfers between devices: 357 us -> none  [advance(): summed = accumulate(lax.all_gather(current, 'rows', axis=0, tiled=True))]
    ppermute x0 -> x35, waiting for transfers between devices: none -> 355 us  [the longest x20 342 us: ring_gather(): earlier.append(lax.ppermute(earlier[-1], axis, up))]
    ppermute x0 -> x35, starting transfers between devices: none -> 90.4 us  [the longest x15 61.7 us: ring_gather(): later.append(lax.ppermute(later[-1], axis, down))]
    while x0 -> x85, local copies, waits for them, and re-layouts: none -> 13.2 us
  transfers between devices with their start and end apart: 10 -> 40, of which waited for: 5 -> 30; matrix products, arithmetic and copies ran while one was open for 2% -> 3% of each run, Pallas kernels for 0% -> 0%
where the time goes in v1:
time: 664 us; the launch traced here: 663 us
  waiting for transfers between devices  355 us (53%)
  matrix products  165 us (25%)
  starting transfers between devices  107 us (16%)
  local copies, waits for them, and re-layouts  34.4 us (5%)
    ppermute x20, waiting for transfers between devices, ring_gather(): earlier.append(lax.ppermute(earlier[-1], axis, up))  342 us
    dot_general x5, matrix products, accumulate(): jnp.einsum('arn,nc->arc', kernel, panel, precision=lax.Precision.HIGHEST,...  164 us
    ppermute x15, starting transfers between devices, ring_gather(): later.append(lax.ppermute(later[-1], axis, down))  61.7 us
    ppermute x20, starting transfers between devices, ring_gather(): earlier.append(lax.ppermute(earlier[-1], axis, up))  28.6 us
    ppermute x5, starting transfers between devices, from_behind(): return lax.ppermute(value, axis, pairs)  16.6 us
  transfers between devices with their start and end apart: 40, of which 30 were waited for; matrix products, arithmetic and copies ran while one was open for 3% of the time, Pallas kernels for 0%

profile of v1, /device:TPU:1, one launch (start us, length us, event | category | flops | bytes accessed | tf_op | source)
XLA Modules:
  0.0 663.0 jit_solution(5300821813988938035)
XLA Ops:
  4.0 659.0 %while.17 = (s32[]{:T(128)}, f32[512,256]{0,1:T(8,128)}, f32[512,1024]{1,0:T(8,128)}, pred[]{:T(512)}, s32[]{:T(128)}, /*index=5*/f32[512,1024]{1,0:T(8,128)}, f...) while((s32[]{:T(128)}, f32[512,256]{0,1:T(8,128)}, ...), condition=%wide.region_2.3_spmd, body=%wide.region_0.2_spmd.sunk | while | flops 25771507712 | bytes 81318760 | solution.py:74
  7.5 13.6 %collective-permute-done = f32[512,256]{0,1:T(8,128)S(1)} collective-permute-done((f32[512,256]{0,1:T(8,128)S(1)}, f32[512,256]{0,1:T(8,128)S(1)}, u32[]{:S(2)}, u32[]{:S(2)}) %collective-permute-start) | collective-permute-done | bytes 524320 | tf_op jit(solution)/shard_map/while/body/eval_jaxpr/ppermute | solution.py:13
  21.0 4.2 collective-permute-start.4
  25.2 17.5 %collective-permute-done.1 = f32[512,256]{0,1:T(8,128)S(1)} collective-permute-done((f32[512,256]{0,1:T(8,128)S(1)}, f32[512,256]{0,1:T(8,128)S(1)}, u32[]{:S(2)}, u32[]{:S(2)}) %collective-permute-start.1) | collective-permute-done | bytes 524320 | tf_op jit(solution)/shard_map/while/body/eval_jaxpr/ppermute | solution.py:13
  42.7 2.2 collective-permute-start.2
  44.9 13.5 %collective-permute-start.5 = (f32[512,256]{0,1:T(8,128)S(1)}, f32[512,256]{0,1:T(8,128)S(1)}, u32[]{:S(2)}, u32[]{:S(2)}) collective-permute-start(f32[512,256]{0,1:T(8,128)S(1)} %collective-permute-done.4), channel_id=1, source_target_pairs={{0,14},{2,0},{4,2},{6,4},{8,6},{10,8},{12,10},{14,12},{1,15},{3,1}... | collective-permute-start | bytes 1572872 | tf_op jit(solution)/shard_map/while/body/eval_jaxpr/ppermute | solution.py:15
  58.4 8.4 %collective-permute-done.2 = f32[512,256]{0,1:T(8,128)S(1)} collective-permute-done((f32[512,256]{0,1:T(8,128)S(1)}, f32[512,256]{0,1:T(8,128)S(1)}, u32[]{:S(2)}, u32[]{:S(2)}) %collective-permute-start.2) | collective-permute-done | bytes 524320 | tf_op jit(solution)/shard_map/while/body/eval_jaxpr/ppermute | solution.py:13
  66.7 2.2 collective-permute-start.3
  69.4 13.2 %collective-permute-start.6 = (f32[512,256]{0,1:T(8,128)S(1)}, f32[512,256]{0,1:T(8,128)S(1)}, u32[]{:S(2)}, u32[]{:S(2)}) collective-permute-start(f32[512,256]{0,1:T(8,128)S(1)} %collective-permute-done.5), channel_id=1, source_target_pairs={{0,14},{2,0},{4,2},{6,4},{8,6},{10,8},{12,10},{14,12},{1,15},{3,1}... | collective-permute-start | bytes 1572872 | tf_op jit(solution)/shard_map/while/body/eval_jaxpr/ppermute | solution.py:15
  82.6 8.2 %collective-permute-done.3 = f32[512,256]{0,1:T(8,128)} collective-permute-done((f32[512,256]{0,1:T(8,128)S(1)}, f32[512,256]{0,1:T(8,128)}, u32[]{:S(2)}, u32[]{:S(2)}) %collective-permute-start.3) | collective-permute-done | bytes 524320 | tf_op jit(solution)/shard_map/while/body/eval_jaxpr/ppermute | solution.py:13
  92.1 2.3 collective-permute-done.6
  95.9 32.8 %fusion.15 = f32[512,256]{0,1:T(8,128)S(1)} fusion(f32[4,512,4096]{2,1,0:T(8,128)} %get-tuple-element.372, f32[8192,256]{0,1:T(8,128)S(1)} %constant_dynamic-update-slice_fusion.49, s32[]{:T(128)S(6)} %select_n.105, f32[4,256]{1,0:T(4,128)S(1)} %constant_dynamic-slice_fusion.7, f32[4,512]{1,0:T(4,128)S(1)} %bitcast.27), kind=kOutput, calls=%fused_computation.4.clone.1 | convolution fusion | flops 25771245568 | bytes 38285316 | tf_op jit(solution)/shard_map/while/body/eval_jaxpr/arn,nc->arc/dot_general | solution.py:42
  128.7 3.2 collective-permute-start.7
  136.8 16.1 %collective-permute-done = f32[512,256]{0,1:T(8,128)S(1)} collective-permute-done((f32[512,256]{0,1:T(8,128)S(1)}, f32[512,256]{0,1:T(8,128)S(1)}, u32[]{:S(2)}, u32[]{:S(2)}) %collective-permute-start) | collective-permute-done | bytes 524320 | tf_op jit(solution)/shard_map/while/body/eval_jaxpr/ppermute | solution.py:13
  153.0 4.2 collective-permute-start.4
  157.1 18.4 %collective-permute-done.1 = f32[512,256]{0,1:T(8,128)S(1)} collective-permute-done((f32[512,256]{0,1:T(8,128)S(1)}, f32[512,256]{0,1:T(8,128)S(1)}, u32[]{:S(2)}, u32[]{:S(2)}) %collective-permute-start.1) | collective-permute-done | bytes 524320 | tf_op jit(solution)/shard_map/while/body/eval_jaxpr/ppermute | solution.py:13
  175.5 2.2 collective-permute-start.2
  179.7 20.1 %collective-permute-done.2 = f32[512,256]{0,1:T(8,128)S(1)} collective-permute-done((f32[512,256]{0,1:T(8,128)S(1)}, f32[512,256]{0,1:T(8,128)S(1)}, u32[]{:S(2)}, u32[]{:S(2)}) %collective-permute-start.2) | collective-permute-done | bytes 524320 | tf_op jit(solution)/shard_map/while/body/eval_jaxpr/ppermute | solution.py:13
  199.8 2.2 collective-permute-start.3
  203.9 19.9 %collective-permute-done.3 = f32[512,256]{0,1:T(8,128)} collective-permute-done((f32[512,256]{0,1:T(8,128)S(1)}, f32[512,256]{0,1:T(8,128)}, u32[]{:S(2)}, u32[]{:S(2)}) %collective-permute-start.3) | collective-permute-done | bytes 524320 | tf_op jit(solution)/shard_map/while/body/eval_jaxpr/ppermute | solution.py:13
  228.5 32.8 %fusion.15 = f32[512,256]{0,1:T(8,128)S(1)} fusion(f32[4,512,4096]{2,1,0:T(8,128)} %get-tuple-element.372, f32[8192,256]{0,1:T(8,128)S(1)} %constant_dynamic-update-slice_fusion.49, s32[]{:T(128)S(6)} %select_n.105, f32[4,256]{1,0:T(4,128)S(1)} %constant_dynamic-slice_fusion.7, f32[4,512]{1,0:T(4,128)S(1)} %bitcast.27), kind=kOutput, calls=%fused_computation.4.clone.1 | convolution fusion | flops 25771245568 | bytes 38285316 | tf_op jit(solution)/shard_map/while/body/eval_jaxpr/arn,nc->arc/dot_general | solution.py:42
  261.3 3.4 collective-permute-start.7
  269.9 15.1 %collective-permute-done = f32[512,256]{0,1:T(8,128)S(1)} collective-permute-done((f32[512,256]{0,1:T(8,128)S(1)}, f32[512,256]{0,1:T(8,128)S(1)}, u32[]{:S(2)}, u32[]{:S(2)}) %collective-permute-start) | collective-permute-done | bytes 524320 | tf_op jit(solution)/shard_map/while/body/eval_jaxpr/ppermute | solution.py:13
  285.0 4.2 collective-permute-start.4
  289.2 18.1 %collective-permute-done.1 = f32[512,256]{0,1:T(8,128)S(1)} collective-permute-done((f32[512,256]{0,1:T(8,128)S(1)}, f32[512,256]{0,1:T(8,128)S(1)}, u32[]{:S(2)}, u32[]{:S(2)}) %collective-permute-start.1) | collective-permute-done | bytes 524320 | tf_op jit(solution)/shard_map/while/body/eval_jaxpr/ppermute | solution.py:13
  307.3 2.2 collective-permute-start.2
  311.5 19.9 %collective-permute-done.2 = f32[512,256]{0,1:T(8,128)S(1)} collective-permute-done((f32[512,256]{0,1:T(8,128)S(1)}, f32[512,256]{0,1:T(8,128)S(1)}, u32[]{:S(2)}, u32[]{:S(2)}) %collective-permute-start.2) | collective-permute-done | bytes 524320 | tf_op jit(solution)/shard_map/while/body/eval_jaxpr/ppermute | solution.py:13
  331.4 2.2 collective-permute-start.3
  335.6 19.9 %collective-permute-done.3 = f32[512,256]{0,1:T(8,128)} collective-permute-done((f32[512,256]{0,1:T(8,128)S(1)}, f32[512,256]{0,1:T(8,128)}, u32[]{:S(2)}, u32[]{:S(2)}) %collective-permute-start.3) | collective-permute-done | bytes 524320 | tf_op jit(solution)/shard_map/while/body/eval_jaxpr/ppermute | solution.py:13
  356.8 2.2 collective-permute-done.6
  360.5 32.8 %fusion.15 = f32[512,256]{0,1:T(8,128)S(1)} fusion(f32[4,512,4096]{2,1,0:T(8,128)} %get-tuple-element.372, f32[8192,256]{0,1:T(8,128)S(1)} %constant_dynamic-update-slice_fusion.49, s32[]{:T(128)S(6)} %select_n.105, f32[4,256]{1,0:T(4,128)S(1)} %constant_dynamic-slice_fusion.7, f32[4,512]{1,0:T(4,128)S(1)} %bitcast.27), kind=kOutput, calls=%fused_computation.4.clone.1 | convolution fusion | flops 25771245568 | bytes 38285316 | tf_op jit(solution)/shard_map/while/body/eval_jaxpr/arn,nc->arc/dot_general | solution.py:42
  393.3 3.3 collective-permute-start.7
  401.5 15.3 %collective-permute-done = f32[512,256]{0,1:T(8,128)S(1)} collective-permute-done((f32[512,256]{0,1:T(8,128)S(1)}, f32[512,256]{0,1:T(8,128)S(1)}, u32[]{:S(2)}, u32[]{:S(2)}) %collective-permute-start) | collective-permute-done | bytes 524320 | tf_op jit(solution)/shard_map/while/body/eval_jaxpr/ppermute | solution.py:13
  416.8 4.2 collective-permute-start.4
  421.0 18.3 %collective-permute-done.1 = f32[512,256]{0,1:T(8,128)S(1)} collective-permute-done((f32[512,256]{0,1:T(8,128)S(1)}, f32[512,256]{0,1:T(8,128)S(1)}, u32[]{:S(2)}, u32[]{:S(2)}) %collective-permute-start.1) | collective-permute-done | bytes 524320 | tf_op jit(solution)/shard_map/while/body/eval_jaxpr/ppermute | solution.py:13
  439.3 2.2 collective-permute-start.2
  443.5 20.0 %collective-permute-done.2 = f32[512,256]{0,1:T(8,128)S(1)} collective-permute-done((f32[512,256]{0,1:T(8,128)S(1)}, f32[512,256]{0,1:T(8,128)S(1)}, u32[]{:S(2)}, u32[]{:S(2)}) %collective-permute-start.2) | collective-permute-done | bytes 524320 | tf_op jit(solution)/shard_map/while/body/eval_jaxpr/ppermute | solution.py:13
  463.4 2.2 collective-permute-start.3
  467.6 19.9 %collective-permute-done.3 = f32[512,256]{0,1:T(8,128)} collective-permute-done((f32[512,256]{0,1:T(8,128)S(1)}, f32[512,256]{0,1:T(8,128)}, u32[]{:S(2)}, u32[]{:S(2)}) %collective-permute-start.3) | collective-permute-done | bytes 524320 | tf_op jit(solution)/shard_map/while/body/eval_jaxpr/ppermute | solution.py:13
  492.5 32.8 %fusion.15 = f32[512,256]{0,1:T(8,128)S(1)} fusion(f32[4,512,4096]{2,1,0:T(8,128)} %get-tuple-element.372, f32[8192,256]{0,1:T(8,128)S(1)} %constant_dynamic-update-slice_fusion.49, s32[]{:T(128)S(6)} %select_n.105, f32[4,256]{1,0:T(4,128)S(1)} %constant_dynamic-slice_fusion.7, f32[4,512]{1,0:T(4,128)S(1)} %bitcast.27), kind=kOutput, calls=%fused_computation.4.clone.1 | convolution fusion | flops 25771245568 | bytes 38285316 | tf_op jit(solution)/shard_map/while/body/eval_jaxpr/arn,nc->arc/dot_general | solution.py:42
  525.3 3.3 collective-permute-start.7
  533.5 15.3 %collective-permute-done = f32[512,256]{0,1:T(8,128)S(1)} collective-permute-done((f32[512,256]{0,1:T(8,128)S(1)}, f32[512,256]{0,1:T(8,128)S(1)}, u32[]{:S(2)}, u32[]{:S(2)}) %collective-permute-start) | collective-permute-done | bytes 524320 | tf_op jit(solution)/shard_map/while/body/eval_jaxpr/ppermute | solution.py:13
  548.8 4.2 collective-permute-start.4
  553.0 18.3 %collective-permute-done.1 = f32[512,256]{0,1:T(8,128)S(1)} collective-permute-done((f32[512,256]{0,1:T(8,128)S(1)}, f32[512,256]{0,1:T(8,128)S(1)}, u32[]{:S(2)}, u32[]{:S(2)}) %collective-permute-start.1) | collective-permute-done | bytes 524320 | tf_op jit(solution)/shard_map/while/body/eval_jaxpr/ppermute | solution.py:13
  575.4 20.0 %collective-permute-done.2 = f32[512,256]{0,1:T(8,128)S(1)} collective-permute-done((f32[512,256]{0,1:T(8,128)S(1)}, f32[512,256]{0,1:T(8,128)S(1)}, u32[]{:S(2)}, u32[]{:S(2)}) %collective-permute-start.2) | collective-permute-done | bytes 524320 | tf_op jit(solution)/shard_map/while/body/eval_jaxpr/ppermute | solution.py:13
  599.6 19.9 %collective-permute-done.3 = f32[512,256]{0,1:T(8,128)} collective-permute-done((f32[512,256]{0,1:T(8,128)S(1)}, f32[512,256]{0,1:T(8,128)}, u32[]{:S(2)}, u32[]{:S(2)}) %collective-permute-start.3) | collective-permute-done | bytes 524320 | tf_op jit(solution)/shard_map/while/body/eval_jaxpr/ppermute | solution.py:13
  624.4 32.8 %fusion.15 = f32[512,256]{0,1:T(8,128)S(1)} fusion(f32[4,512,4096]{2,1,0:T(8,128)} %get-tuple-element.372, f32[8192,256]{0,1:T(8,128)S(1)} %constant_dynamic-update-slice_fusion.49, s32[]{:T(128)S(6)} %select_n.105, f32[4,256]{1,0:T(4,128)S(1)} %constant_dynamic-slice_fusion.7, f32[4,512]{1,0:T(4,128)S(1)} %bitcast.27), kind=kOutput, calls=%fused_computation.4.clone.1 | convolution fusion | flops 25771245568 | bytes 38285316 | tf_op jit(solution)/shard_map/while/body/eval_jaxpr/arn,nc->arc/dot_general | solution.py:42
  657.3 3.3 collective-permute-start.7
  (178 shorter events, 69.8 us)
Async XLA Ops:
  0.0 0.7 copy-start
  5.4 15.7 %collective-permute-start = (f32[512,256]{0,1:T(8,128)S(1)}, f32[512,256]{0,1:T(8,128)S(1)}, u32[]{:S(2)}, u32[]{:S(2)}) collective-permute-start(f32[512,256]{0,1:T(8,128)S(1)} %broadcast_select_fusion.4), channel_id=1, source_target_pairs={{0,2},{2,4},{4,6},{6,8},{8,10},{10,12},{12,14},{14,0},{1,3},{3,5},... | collective-permute-start | bytes 1572872 | tf_op jit(solution)/shard_map/while/body/eval_jaxpr/ppermute | solution.py:13
  21.0 21.6 %collective-permute-start.1 = (f32[512,256]{0,1:T(8,128)S(1)}, f32[512,256]{0,1:T(8,128)S(1)}, u32[]{:S(2)}, u32[]{:S(2)}) collective-permute-start(f32[512,256]{0,1:T(8,128)S(1)} %collective-permute-done), channel_id=1, source_target_pairs={{0,2},{2,4},{4,6},{6,8},{8,10},{10,12},{12,14},{14,0},{1,3},{3,5},... | collective-permute-start | bytes 1572872 | tf_op jit(solution)/shard_map/while/body/eval_jaxpr/ppermute | solution.py:13
  21.0 23.8 %collective-permute-start.4 = (f32[512,256]{0,1:T(8,128)S(1)}, f32[512,256]{0,1:T(8,128)S(1)}, u32[]{:S(2)}, u32[]{:S(2)}) collective-permute-start(f32[512,256]{0,1:T(8,128)S(1)} %broadcast_select_fusion.4), channel_id=1, source_target_pairs={{0,14},{2,0},{4,2},{6,4},{8,6},{10,8},{12,10},{14,12},{1,15},{3,1}... | collective-permute-start | bytes 1572872 | tf_op jit(solution)/shard_map/while/body/eval_jaxpr/ppermute | solution.py:15
  42.7 24.1 %collective-permute-start.2 = (f32[512,256]{0,1:T(8,128)S(1)}, f32[512,256]{0,1:T(8,128)S(1)}, u32[]{:S(2)}, u32[]{:S(2)}) collective-permute-start(f32[512,256]{0,1:T(8,128)S(1)} %collective-permute-done.1), channel_id=1, source_target_pairs={{0,2},{2,4},{4,6},{6,8},{8,10},{10,12},{12,14},{14,0},{1,3},{3,5},... | collective-permute-start | bytes 1572872 | tf_op jit(solution)/shard_map/while/body/eval_jaxpr/ppermute | solution.py:13
  44.9 24.5 %collective-permute-start.5 = (f32[512,256]{0,1:T(8,128)S(1)}, f32[512,256]{0,1:T(8,128)S(1)}, u32[]{:S(2)}, u32[]{:S(2)}) collective-permute-start(f32[512,256]{0,1:T(8,128)S(1)} %collective-permute-done.4), channel_id=1, source_target_pairs={{0,14},{2,0},{4,2},{6,4},{8,6},{10,8},{12,10},{14,12},{1,15},{3,1}... | collective-permute-start | bytes 1572872 | tf_op jit(solution)/shard_map/while/body/eval_jaxpr/ppermute | solution.py:15
  66.7 24.0 %collective-permute-start.3 = (f32[512,256]{0,1:T(8,128)S(1)}, f32[512,256]{0,1:T(8,128)}, u32[]{:S(2)}, u32[]{:S(2)}) collective-permute-start(f32[512,256]{0,1:T(8,128)S(1)} %collective-permute-done.2), channel_id=1, source_target_pairs={{0,2},{2,4},{4,6},{6,8},{8,10},{10,12},{12,14},{14,0},{1,3},{3,5},... | collective-permute-start | bytes 1572872 | tf_op jit(solution)/shard_map/while/body/eval_jaxpr/ppermute | solution.py:13
  68.9 27.0 %copy-start.1 = (f32[1,4,512]{2,1,0:T(4,128)S(1)}, f32[1,4,512]{2,1,0:T(4,128)}, u32[]{:S(2)}) copy-start(f32[1,4,512]{2,1,0:T(4,128)} %get-tuple-element.373) | copy-start | bytes 24580 | tf_op jit(solution)/shard_map/while
  69.4 25.1 %collective-permute-start.6 = (f32[512,256]{0,1:T(8,128)S(1)}, f32[512,256]{0,1:T(8,128)S(1)}, u32[]{:S(2)}, u32[]{:S(2)}) collective-permute-start(f32[512,256]{0,1:T(8,128)S(1)} %collective-permute-done.5), channel_id=1, source_target_pairs={{0,14},{2,0},{4,2},{6,4},{8,6},{10,8},{12,10},{14,12},{1,15},{3,1}... | collective-permute-start | bytes 1572872 | tf_op jit(solution)/shard_map/while/body/eval_jaxpr/ppermute | solution.py:15
  128.7 5.7 collective-permute-start.7
  135.8 17.2 %collective-permute-start = (f32[512,256]{0,1:T(8,128)S(1)}, f32[512,256]{0,1:T(8,128)S(1)}, u32[]{:S(2)}, u32[]{:S(2)}) collective-permute-start(f32[512,256]{0,1:T(8,128)S(1)} %broadcast_select_fusion.4), channel_id=1, source_target_pairs={{0,2},{2,4},{4,6},{6,8},{8,10},{10,12},{12,14},{14,0},{1,3},{3,5},... | collective-permute-start | bytes 1572872 | tf_op jit(solution)/shard_map/while/body/eval_jaxpr/ppermute | solution.py:13
  153.0 22.5 %collective-permute-start.1 = (f32[512,256]{0,1:T(8,128)S(1)}, f32[512,256]{0,1:T(8,128)S(1)}, u32[]{:S(2)}, u32[]{:S(2)}) collective-permute-start(f32[512,256]{0,1:T(8,128)S(1)} %collective-permute-done), channel_id=1, source_target_pairs={{0,2},{2,4},{4,6},{6,8},{8,10},{10,12},{12,14},{14,0},{1,3},{3,5},... | collective-permute-start | bytes 1572872 | tf_op jit(solution)/shard_map/while/body/eval_jaxpr/ppermute | solution.py:13
  153.0 24.7 %collective-permute-start.4 = (f32[512,256]{0,1:T(8,128)S(1)}, f32[512,256]{0,1:T(8,128)S(1)}, u32[]{:S(2)}, u32[]{:S(2)}) collective-permute-start(f32[512,256]{0,1:T(8,128)S(1)} %broadcast_select_fusion.4), channel_id=1, source_target_pairs={{0,14},{2,0},{4,2},{6,4},{8,6},{10,8},{12,10},{14,12},{1,15},{3,1}... | collective-permute-start | bytes 1572872 | tf_op jit(solution)/shard_map/while/body/eval_jaxpr/ppermute | solution.py:15
  175.5 24.3 %collective-permute-start.2 = (f32[512,256]{0,1:T(8,128)S(1)}, f32[512,256]{0,1:T(8,128)S(1)}, u32[]{:S(2)}, u32[]{:S(2)}) collective-permute-start(f32[512,256]{0,1:T(8,128)S(1)} %collective-permute-done.1), channel_id=1, source_target_pairs={{0,2},{2,4},{4,6},{6,8},{8,10},{10,12},{12,14},{14,0},{1,3},{3,5},... | collective-permute-start | bytes 1572872 | tf_op jit(solution)/shard_map/while/body/eval_jaxpr/ppermute | solution.py:13
  177.7 24.5 %collective-permute-start.5 = (f32[512,256]{0,1:T(8,128)S(1)}, f32[512,256]{0,1:T(8,128)S(1)}, u32[]{:S(2)}, u32[]{:S(2)}) collective-permute-start(f32[512,256]{0,1:T(8,128)S(1)} %collective-permute-done.4), channel_id=1, source_target_pairs={{0,14},{2,0},{4,2},{6,4},{8,6},{10,8},{12,10},{14,12},{1,15},{3,1}... | collective-permute-start | bytes 1572872 | tf_op jit(solution)/shard_map/while/body/eval_jaxpr/ppermute | solution.py:15
  199.8 24.0 %collective-permute-start.3 = (f32[512,256]{0,1:T(8,128)S(1)}, f32[512,256]{0,1:T(8,128)}, u32[]{:S(2)}, u32[]{:S(2)}) collective-permute-start(f32[512,256]{0,1:T(8,128)S(1)} %collective-permute-done.2), channel_id=1, source_target_pairs={{0,2},{2,4},{4,6},{6,8},{8,10},{10,12},{12,14},{14,0},{1,3},{3,5},... | collective-permute-start | bytes 1572872 | tf_op jit(solution)/shard_map/while/body/eval_jaxpr/ppermute | solution.py:13
  202.0 26.5 %copy-start.1 = (f32[1,4,512]{2,1,0:T(4,128)S(1)}, f32[1,4,512]{2,1,0:T(4,128)}, u32[]{:S(2)}) copy-start(f32[1,4,512]{2,1,0:T(4,128)} %get-tuple-element.373) | copy-start | bytes 24580 | tf_op jit(solution)/shard_map/while
  202.2 24.8 %collective-permute-start.6 = (f32[512,256]{0,1:T(8,128)S(1)}, f32[512,256]{0,1:T(8,128)S(1)}, u32[]{:S(2)}, u32[]{:S(2)}) collective-permute-start(f32[512,256]{0,1:T(8,128)S(1)} %collective-permute-done.5), channel_id=1, source_target_pairs={{0,14},{2,0},{4,2},{6,4},{8,6},{10,8},{12,10},{14,12},{1,15},{3,1}... | collective-permute-start | bytes 1572872 | tf_op jit(solution)/shard_map/while/body/eval_jaxpr/ppermute | solution.py:15
  261.3 5.9 collective-permute-start.7
  268.6 16.4 %collective-permute-start = (f32[512,256]{0,1:T(8,128)S(1)}, f32[512,256]{0,1:T(8,128)S(1)}, u32[]{:S(2)}, u32[]{:S(2)}) collective-permute-start(f32[512,256]{0,1:T(8,128)S(1)} %broadcast_select_fusion.4), channel_id=1, source_target_pairs={{0,2},{2,4},{4,6},{6,8},{8,10},{10,12},{12,14},{14,0},{1,3},{3,5},... | collective-permute-start | bytes 1572872 | tf_op jit(solution)/shard_map/while/body/eval_jaxpr/ppermute | solution.py:13
  285.0 22.3 %collective-permute-start.1 = (f32[512,256]{0,1:T(8,128)S(1)}, f32[512,256]{0,1:T(8,128)S(1)}, u32[]{:S(2)}, u32[]{:S(2)}) collective-permute-start(f32[512,256]{0,1:T(8,128)S(1)} %collective-permute-done), channel_id=1, source_target_pairs={{0,2},{2,4},{4,6},{6,8},{8,10},{10,12},{12,14},{14,0},{1,3},{3,5},... | collective-permute-start | bytes 1572872 | tf_op jit(solution)/shard_map/while/body/eval_jaxpr/ppermute | solution.py:13
  285.0 24.5 %collective-permute-start.4 = (f32[512,256]{0,1:T(8,128)S(1)}, f32[512,256]{0,1:T(8,128)S(1)}, u32[]{:S(2)}, u32[]{:S(2)}) collective-permute-start(f32[512,256]{0,1:T(8,128)S(1)} %broadcast_select_fusion.4), channel_id=1, source_target_pairs={{0,14},{2,0},{4,2},{6,4},{8,6},{10,8},{12,10},{14,12},{1,15},{3,1}... | collective-permute-start | bytes 1572872 | tf_op jit(solution)/shard_map/while/body/eval_jaxpr/ppermute | solution.py:15
  307.3 24.1 %collective-permute-start.2 = (f32[512,256]{0,1:T(8,128)S(1)}, f32[512,256]{0,1:T(8,128)S(1)}, u32[]{:S(2)}, u32[]{:S(2)}) collective-permute-start(f32[512,256]{0,1:T(8,128)S(1)} %collective-permute-done.1), channel_id=1, source_target_pairs={{0,2},{2,4},{4,6},{6,8},{8,10},{10,12},{12,14},{14,0},{1,3},{3,5},... | collective-permute-start | bytes 1572872 | tf_op jit(solution)/shard_map/while/body/eval_jaxpr/ppermute | solution.py:13
  309.5 24.5 %collective-permute-start.5 = (f32[512,256]{0,1:T(8,128)S(1)}, f32[512,256]{0,1:T(8,128)S(1)}, u32[]{:S(2)}, u32[]{:S(2)}) collective-permute-start(f32[512,256]{0,1:T(8,128)S(1)} %collective-permute-done.4), channel_id=1, source_target_pairs={{0,14},{2,0},{4,2},{6,4},{8,6},{10,8},{12,10},{14,12},{1,15},{3,1}... | collective-permute-start | bytes 1572872 | tf_op jit(solution)/shard_map/while/body/eval_jaxpr/ppermute | solution.py:15
  331.4 24.0 %collective-permute-start.3 = (f32[512,256]{0,1:T(8,128)S(1)}, f32[512,256]{0,1:T(8,128)}, u32[]{:S(2)}, u32[]{:S(2)}) collective-permute-start(f32[512,256]{0,1:T(8,128)S(1)} %collective-permute-done.2), channel_id=1, source_target_pairs={{0,2},{2,4},{4,6},{6,8},{8,10},{10,12},{12,14},{14,0},{1,3},{3,5},... | collective-permute-start | bytes 1572872 | tf_op jit(solution)/shard_map/while/body/eval_jaxpr/ppermute | solution.py:13
  333.6 26.9 %copy-start.1 = (f32[1,4,512]{2,1,0:T(4,128)S(1)}, f32[1,4,512]{2,1,0:T(4,128)}, u32[]{:S(2)}) copy-start(f32[1,4,512]{2,1,0:T(4,128)} %get-tuple-element.373) | copy-start | bytes 24580 | tf_op jit(solution)/shard_map/while
  334.1 25.0 %collective-permute-start.6 = (f32[512,256]{0,1:T(8,128)S(1)}, f32[512,256]{0,1:T(8,128)S(1)}, u32[]{:S(2)}, u32[]{:S(2)}) collective-permute-start(f32[512,256]{0,1:T(8,128)S(1)} %collective-permute-done.5), channel_id=1, source_target_pairs={{0,14},{2,0},{4,2},{6,4},{8,6},{10,8},{12,10},{14,12},{1,15},{3,1}... | collective-permute-start | bytes 1572872 | tf_op jit(solution)/shard_map/while/body/eval_jaxpr/ppermute | solution.py:15
  393.3 5.7 collective-permute-start.7
  400.4 16.4 %collective-permute-start = (f32[512,256]{0,1:T(8,128)S(1)}, f32[512,256]{0,1:T(8,128)S(1)}, u32[]{:S(2)}, u32[]{:S(2)}) collective-permute-start(f32[512,256]{0,1:T(8,128)S(1)} %broadcast_select_fusion.4), channel_id=1, source_target_pairs={{0,2},{2,4},{4,6},{6,8},{8,10},{10,12},{12,14},{14,0},{1,3},{3,5},... | collective-permute-start | bytes 1572872 | tf_op jit(solution)/shard_map/while/body/eval_jaxpr/ppermute | solution.py:13
  416.8 22.5 %collective-permute-start.1 = (f32[512,256]{0,1:T(8,128)S(1)}, f32[512,256]{0,1:T(8,128)S(1)}, u32[]{:S(2)}, u32[]{:S(2)}) collective-permute-start(f32[512,256]{0,1:T(8,128)S(1)} %collective-permute-done), channel_id=1, source_target_pairs={{0,2},{2,4},{4,6},{6,8},{8,10},{10,12},{12,14},{14,0},{1,3},{3,5},... | collective-permute-start | bytes 1572872 | tf_op jit(solution)/shard_map/while/body/eval_jaxpr/ppermute | solution.py:13
  416.8 24.7 %collective-permute-start.4 = (f32[512,256]{0,1:T(8,128)S(1)}, f32[512,256]{0,1:T(8,128)S(1)}, u32[]{:S(2)}, u32[]{:S(2)}) collective-permute-start(f32[512,256]{0,1:T(8,128)S(1)} %broadcast_select_fusion.4), channel_id=1, source_target_pairs={{0,14},{2,0},{4,2},{6,4},{8,6},{10,8},{12,10},{14,12},{1,15},{3,1}... | collective-permute-start | bytes 1572872 | tf_op jit(solution)/shard_map/while/body/eval_jaxpr/ppermute | solution.py:15
  439.3 24.1 %collective-permute-start.2 = (f32[512,256]{0,1:T(8,128)S(1)}, f32[512,256]{0,1:T(8,128)S(1)}, u32[]{:S(2)}, u32[]{:S(2)}) collective-permute-start(f32[512,256]{0,1:T(8,128)S(1)} %collective-permute-done.1), channel_id=1, source_target_pairs={{0,2},{2,4},{4,6},{6,8},{8,10},{10,12},{12,14},{14,0},{1,3},{3,5},... | collective-permute-start | bytes 1572872 | tf_op jit(solution)/shard_map/while/body/eval_jaxpr/ppermute | solution.py:13
  441.5 24.5 %collective-permute-start.5 = (f32[512,256]{0,1:T(8,128)S(1)}, f32[512,256]{0,1:T(8,128)S(1)}, u32[]{:S(2)}, u32[]{:S(2)}) collective-permute-start(f32[512,256]{0,1:T(8,128)S(1)} %collective-permute-done.4), channel_id=1, source_target_pairs={{0,14},{2,0},{4,2},{6,4},{8,6},{10,8},{12,10},{14,12},{1,15},{3,1}... | collective-permute-start | bytes 1572872 | tf_op jit(solution)/shard_map/while/body/eval_jaxpr/ppermute | solution.py:15
  463.4 24.0 %collective-permute-start.3 = (f32[512,256]{0,1:T(8,128)S(1)}, f32[512,256]{0,1:T(8,128)}, u32[]{:S(2)}, u32[]{:S(2)}) collective-permute-start(f32[512,256]{0,1:T(8,128)S(1)} %collective-permute-done.2), channel_id=1, source_target_pairs={{0,2},{2,4},{4,6},{6,8},{8,10},{10,12},{12,14},{14,0},{1,3},{3,5},... | collective-permute-start | bytes 1572872 | tf_op jit(solution)/shard_map/while/body/eval_jaxpr/ppermute | solution.py:13
  465.6 26.8 %copy-start.1 = (f32[1,4,512]{2,1,0:T(4,128)S(1)}, f32[1,4,512]{2,1,0:T(4,128)}, u32[]{:S(2)}) copy-start(f32[1,4,512]{2,1,0:T(4,128)} %get-tuple-element.373) | copy-start | bytes 24580 | tf_op jit(solution)/shard_map/while
  466.0 25.0 %collective-permute-start.6 = (f32[512,256]{0,1:T(8,128)S(1)}, f32[512,256]{0,1:T(8,128)S(1)}, u32[]{:S(2)}, u32[]{:S(2)}) collective-permute-start(f32[512,256]{0,1:T(8,128)S(1)} %collective-permute-done.5), channel_id=1, source_target_pairs={{0,14},{2,0},{4,2},{6,4},{8,6},{10,8},{12,10},{14,12},{1,15},{3,1}... | collective-permute-start | bytes 1572872 | tf_op jit(solution)/shard_map/while/body/eval_jaxpr/ppermute | solution.py:15
  525.3 5.7 collective-permute-start.7
  532.4 16.4 %collective-permute-start = (f32[512,256]{0,1:T(8,128)S(1)}, f32[512,256]{0,1:T(8,128)S(1)}, u32[]{:S(2)}, u32[]{:S(2)}) collective-permute-start(f32[512,256]{0,1:T(8,128)S(1)} %broadcast_select_fusion.4), channel_id=1, source_target_pairs={{0,2},{2,4},{4,6},{6,8},{8,10},{10,12},{12,14},{14,0},{1,3},{3,5},... | collective-permute-start | bytes 1572872 | tf_op jit(solution)/shard_map/while/body/eval_jaxpr/ppermute | solution.py:13
  548.8 22.5 %collective-permute-start.1 = (f32[512,256]{0,1:T(8,128)S(1)}, f32[512,256]{0,1:T(8,128)S(1)}, u32[]{:S(2)}, u32[]{:S(2)}) collective-permute-start(f32[512,256]{0,1:T(8,128)S(1)} %collective-permute-done), channel_id=1, source_target_pairs={{0,2},{2,4},{4,6},{6,8},{8,10},{10,12},{12,14},{14,0},{1,3},{3,5},... | collective-permute-start | bytes 1572872 | tf_op jit(solution)/shard_map/while/body/eval_jaxpr/ppermute | solution.py:13
  548.8 24.7 %collective-permute-start.4 = (f32[512,256]{0,1:T(8,128)S(1)}, f32[512,256]{0,1:T(8,128)S(1)}, u32[]{:S(2)}, u32[]{:S(2)}) collective-permute-start(f32[512,256]{0,1:T(8,128)S(1)} %broadcast_select_fusion.4), channel_id=1, source_target_pairs={{0,14},{2,0},{4,2},{6,4},{8,6},{10,8},{12,10},{14,12},{1,15},{3,1}... | collective-permute-start | bytes 1572872 | tf_op jit(solution)/shard_map/while/body/eval_jaxpr/ppermute | solution.py:15
  571.3 24.1 %collective-permute-start.2 = (f32[512,256]{0,1:T(8,128)S(1)}, f32[512,256]{0,1:T(8,128)S(1)}, u32[]{:S(2)}, u32[]{:S(2)}) collective-permute-start(f32[512,256]{0,1:T(8,128)S(1)} %collective-permute-done.1), channel_id=1, source_target_pairs={{0,2},{2,4},{4,6},{6,8},{8,10},{10,12},{12,14},{14,0},{1,3},{3,5},... | collective-permute-start | bytes 1572872 | tf_op jit(solution)/shard_map/while/body/eval_jaxpr/ppermute | solution.py:13
  573.5 24.5 %collective-permute-start.5 = (f32[512,256]{0,1:T(8,128)S(1)}, f32[512,256]{0,1:T(8,128)S(1)}, u32[]{:S(2)}, u32[]{:S(2)}) collective-permute-start(f32[512,256]{0,1:T(8,128)S(1)} %collective-permute-done.4), channel_id=1, source_target_pairs={{0,14},{2,0},{4,2},{6,4},{8,6},{10,8},{12,10},{14,12},{1,15},{3,1}... | collective-permute-start | bytes 1572872 | tf_op jit(solution)/shard_map/while/body/eval_jaxpr/ppermute | solution.py:15
  595.4 24.0 %collective-permute-start.3 = (f32[512,256]{0,1:T(8,128)S(1)}, f32[512,256]{0,1:T(8,128)}, u32[]{:S(2)}, u32[]{:S(2)}) collective-permute-start(f32[512,256]{0,1:T(8,128)S(1)} %collective-permute-done.2), channel_id=1, source_target_pairs={{0,2},{2,4},{4,6},{6,8},{8,10},{10,12},{12,14},{14,0},{1,3},{3,5},... | collective-permute-start | bytes 1572872 | tf_op jit(solution)/shard_map/while/body/eval_jaxpr/ppermute | solution.py:13
  597.6 26.8 %copy-start.1 = (f32[1,4,512]{2,1,0:T(4,128)S(1)}, f32[1,4,512]{2,1,0:T(4,128)}, u32[]{:S(2)}) copy-start(f32[1,4,512]{2,1,0:T(4,128)} %get-tuple-element.373) | copy-start | bytes 24580 | tf_op jit(solution)/shard_map/while
  598.0 25.0 %collective-permute-start.6 = (f32[512,256]{0,1:T(8,128)S(1)}, f32[512,256]{0,1:T(8,128)S(1)}, u32[]{:S(2)}, u32[]{:S(2)}) collective-permute-start(f32[512,256]{0,1:T(8,128)S(1)} %collective-permute-done.5), channel_id=1, source_target_pairs={{0,14},{2,0},{4,2},{6,4},{8,6},{10,8},{12,10},{14,12},{1,15},{3,1}... | collective-permute-start | bytes 1572872 | tf_op jit(solution)/shard_map/while/body/eval_jaxpr/ppermute | solution.py:15
  657.3 5.7 collective-permute-start.7
